TPU v7x, 32 devices: a whole 2x2x4 slice. The times are simulated.
32 devices in a mesh: dom: 8 (over y, x, core), sub: 4 (over z).
Axes of the slice: x: 2, y: 2, z: 4, core: 2. Of those that a mesh axis runs over, the one named last changes fastest.
Arguments:
- upstream: bfloat16 [65536, 128], P(('dom', 'sub')), may hold values from -6 to 6
- features: bfloat16 [65536, 128], P(('dom', 'sub')), may hold values from -6 to 6
- w_in: bfloat16 [128, 128], replicated, may hold values from -0.5 to 0.5
- w_out: bfloat16 [128, 128], replicated, may hold values from -0.5 to 0.5
- inner_adj: bfloat16 [65536, 2048], P(('dom', 'sub')), may hold values from -0.125 to 0.125
- cut_tiles: bfloat16 [768, 128, 128], P(('dom', 'sub')), may hold values from -0.15625 to 0.15625
- cut_list: int32 [768, 3], P(('dom', 'sub')), may hold values from 0 to 511, as said below
- cut_count: int32 [32], P(('dom', 'sub')), may hold values from 1 to 24, as said below
Outputs:
- input_grad: bfloat16 [65536, 128], P(('dom', 'sub'))
- grad_w_in: float32 [128, 128], replicated
- grad_w_out: float32 [128, 128], replicated
Inputs may be any that keep to these rules, and one draw needn't show every extreme that they name: `cut_list`: device s's list has 24 rows; column 0 is a local block below 16, column 1 a global block whose device is not s, column 2 a tile id below 24, all tile ids of one device distinct. Among the first cut_count[s] rows the devices of column 1 are all distinct, so one device sends at most one block to another. `cut_count`: some device has exactly 24 live entries in every draw.
All inputs are finite; a program needn't handle non-finite values.
Results may differ from a plain program's by a relative error of at most 0.015.
Values may be sent and summed in bfloat16 or wider, within the bound.
A program may use at most 128 MiB of HBM per device.

v0:
```python
import math

import jax
import jax.numpy as jnp
from jax import lax
from jax.sharding import PartitionSpec as P

STEPS = 4


teleport = 0.1


def on_device(upstream, features, w_in, w_out, inner_adj, cut_tiles, cut_list, cut_count):
    local_rows = upstream.shape[0]
    feature_width = upstream.shape[1]
    block_rows = cut_tiles.shape[1]
    block_count = local_rows // block_rows
    entry_count = cut_list.shape[0]
    dom_size = lax.axis_size("dom")
    sub_size = lax.axis_size("sub")
    device_count = dom_size * sub_size
    total_rows = local_rows * device_count
    live_count = cut_count[0]
    read_block = cut_list[:, 0]
    target_device = cut_list[:, 1] // block_count
    target_block = cut_list[:, 1] % block_count
    entry_tiles = cut_tiles[cut_list[:, 2]]
    entry_index = jnp.arange(entry_count, dtype=jnp.int32)
    live = entry_index < live_count
    slot_block = (
        jnp.zeros((device_count, 1), jnp.int32)
        .at[target_device, 0]
        .add(jnp.where(live, target_block, 0))
    )
    block_ids = jnp.arange(block_count, dtype=jnp.int32)
    empty_buffer = jnp.zeros((device_count, block_rows, feature_width), jnp.bfloat16)
    vector = upstream
    accum = jnp.zeros((local_rows, feature_width), jnp.float32)
    for section_index in range(STEPS):
        accum = accum + teleport * vector.astype(jnp.float32)
        local_term = jnp.dot(inner_adj, vector, preferred_element_type=jnp.float32)
        chosen = vector.reshape(block_count, block_rows, feature_width)[read_block]
        products = jnp.einsum(
            "cij,cjk->cik", entry_tiles, chosen, preferred_element_type=jnp.float32
        )
        products = jnp.where(live[:, None, None], products, 0.0).astype(jnp.bfloat16)
        outbound = empty_buffer.at[target_device].add(products)
        arrived = lax.all_to_all(outbound, ("dom", "sub"), split_axis=0, concat_axis=0, tiled=True)
        arrived_slot = lax.all_to_all(
            slot_block, ("dom", "sub"), split_axis=0, concat_axis=0, tiled=True
        )
        selector = (arrived_slot[:, 0][None, :] == block_ids[:, None]).astype(jnp.bfloat16)
        flat_arrived = arrived.reshape(device_count, block_rows * feature_width)
        cut_term = jnp.dot(selector, flat_arrived, preferred_element_type=jnp.float32)
        cut_term = cut_term.reshape(local_rows, feature_width)
        vector = ((1.0 - teleport) * (local_term + cut_term)).astype(jnp.bfloat16)
    head_grad = (accum + vector.astype(jnp.float32)).astype(jnp.bfloat16)
    pre = jnp.dot(features, w_in, preferred_element_type=jnp.float32)
    gate = jax.nn.sigmoid(pre)
    act = (pre * gate).astype(jnp.bfloat16)
    norm_scale = 1.0 / math.sqrt(total_rows)
    part_out = (
        jnp.einsum("rh,re->he", act, head_grad, preferred_element_type=jnp.float32) * norm_scale
    )
    back = jnp.dot(head_grad, w_out.T, preferred_element_type=jnp.float32)
    dpre = (back * gate * (1.0 + pre * (1.0 - gate))).astype(jnp.bfloat16)
    part_in = (
        jnp.einsum("rf,rh->fh", features, dpre, preferred_element_type=jnp.float32) * norm_scale
    )
    input_grad = jnp.dot(dpre, w_in.T, preferred_element_type=jnp.float32).astype(jnp.bfloat16)
    totals = lax.psum((part_in, part_out), ("dom", "sub"))
    return (input_grad, totals[0], totals[1])


def solution(mesh):
    placed = (
        P(("dom", "sub"), None),
        P(("dom", "sub"), None),
        P(),
        P(),
        P(("dom", "sub"), None),
        P(("dom", "sub"), None, None),
        P(("dom", "sub"), None),
        P(("dom", "sub")),
    )
    return jax.shard_map(
        on_device,
        mesh=mesh,
        in_specs=placed,
        out_specs=(P(("dom", "sub"), None), P(), P()),
        check_vma=False,
    )
```

profile of v0, /device:TPU:0, one launch (start us, length us, event | category | flops | bytes accessed | tf_op | source)
XLA Modules:
  0.0 340.4 jit_solution(13540368065045561766)
XLA Ops:
  7.2 0.8 fusion.37
  8.6 0.7 fusion.33
  9.3 0.7 scatter_custom_fusion
  10.0 0.7 copy.20
  10.7 7.3 %all-to-all-start = ((s32[32,1,1]{2,1,0:T(1,128)}), s32[32,1,1]{2,1,0:T(1,128)S(1)}, u32[]{:S(2)}, u32[]{:S(2)}) async-start(s32[32,1,1]{2,1,0:T(1,128)} %copy.20), calls=%async_computation | async-start | bytes 32768 | tf_op jit(solution)/shard_map/all_to_all | solution.py:50
  18.1 0.7 gather_fusion
  18.8 1.7 gather_fusion.1
  20.6 0.4 select_convert_fusion.3
  20.9 1.2 broadcast_in_dim.51.clone.2
  22.2 6.6 %scatter_fusion = bf16[32,128,128]{2,1,0:T(8,128)(2,1)} fusion(bf16[32,128,128]{2,1,0:T(8,128)(2,1)} %broadcast_in_dim.51.clone.2, s32[24]{0:T(128)S(1)} %get-tuple-element.15, bf16[24,128,128]{2,1,0:T(8,128)(2,1)S(1)} %select_convert_fusion.3), kind=kCustom, calls=%fused_computation.6 | custom fusion | flops 393216 | bytes 2359392 | tf_op jit(solution)/shard_map/scatter-add | solution.py:48
  28.8 5.8 %all-to-all-start.1 = ((bf16[32,128,128]{2,1,0:T(8,128)(2,1)}), bf16[32,128,128]{2,1,0:T(8,128)(2,1)S(1)}, u32[]{:S(2)}, u32[]{:S(2)}) async-start(bf16[32,128,128]{2,1,0:T(8,128)(2,1)} %scatter_fusion), calls=%async_computation.1 | async-start | bytes 2097152 | tf_op jit(solution)/shard_map/all_to_all | solution.py:49
  34.6 0.7 reduce
  35.2 24.3 %all-to-all-done.1 = bf16[32,128,128]{2,1,0:T(8,128)(2,1)S(1)} async-done(((bf16[32,128,128]{2,1,0:T(8,128)(2,1)}), bf16[32,128,128]{2,1,0:T(8,128)(2,1)S(1)}, u32[]{:S(2)}, u32[]{:S(2)}) %all-to-all-start.1) | async-done | bytes 1048608 | tf_op jit(solution)/shard_map/all_to_all | solution.py:49
  59.5 1.6 fusion.26
  61.1 1.4 reshape.52
  62.5 6.5 %fusion.9 = bf16[2048,128]{1,0:T(8,128)(2,1)} fusion(f32[2048,128]{1,0:T(8,128)S(1)} %reshape.52, bf16[2048,2048]{1,0:T(8,128)(2,1)} %param.12, bf16[2048,128]{1,0:T(8,128)(2,1)S(1)} %copy-done.2), kind=kOutput, calls=%fused_computation.25 | convolution fusion | flops 1074528256 | bytes 10485760 | tf_op jit(solution)/shard_map/dot_general | solution.py:42
  69.0 1.7 gather_fusion.2
  70.8 0.4 select_convert_fusion.2
  71.4 3.6 %scatter_fusion.1 = bf16[32,128,128]{2,1,0:T(8,128)(2,1)S(1)} fusion(bf16[32,128,128]{2,1,0:T(8,128)(2,1)S(1)} %broadcast_in_dim.51.clone.1, s32[24]{0:T(128)S(1)} %get-tuple-element.15, bf16[24,128,128]{2,1,0:T(8,128)(2,1)S(1)} %select_convert_fusion.2), kind=kCustom, calls=%fused_computation.7 | custom fusion | flops 393216 | bytes 2359392 | tf_op jit(solution)/shard_map/scatter-add | solution.py:48
  75.0 29.3 %all_to_all.32 = bf16[32,128,128]{2,1,0:T(8,128)(2,1)S(1)} all-to-all(bf16[32,128,128]{2,1,0:T(8,128)(2,1)S(1)} %scatter_fusion.1), channel_id=1, replica_groups=mesh['dom'=8,'sub'=4] {'dom','sub'}, dimensions={0} | all-to-all | bytes 2097152 | tf_op jit(solution)/shard_map/all_to_all | solution.py:49
  104.3 0.7 fusion.23
  105.0 1.1 reshape.55
  106.1 6.1 %fusion.15 = bf16[2048,128]{1,0:T(8,128)(2,1)S(1)} fusion(f32[2048,128]{1,0:T(8,128)} %reshape.55, bf16[2048,2048]{1,0:T(8,128)(2,1)} %param.12, bf16[2048,128]{1,0:T(8,128)(2,1)} %fusion.9), kind=kOutput, calls=%fused_computation.31 | convolution fusion | flops 1074528256 | bytes 10485760 | tf_op jit(solution)/shard_map/dot_general | solution.py:42
  112.2 0.8 copy-done.3
  113.0 0.7 gather_fusion.3
  114.3 3.6 %scatter_fusion.2 = bf16[32,128,128]{2,1,0:T(8,128)(2,1)S(1)} fusion(bf16[32,128,128]{2,1,0:T(8,128)(2,1)S(1)} %broadcast_in_dim.51.clone, s32[24]{0:T(128)S(1)} %get-tuple-element.15, bf16[24,128,128]{2,1,0:T(8,128)(2,1)S(1)} %select_convert_fusion.1), kind=kCustom, calls=%fused_computation.8 | custom fusion | flops 393216 | bytes 2359392 | tf_op jit(solution)/shard_map/scatter-add | solution.py:48
  117.9 29.3 %all_to_all.33 = bf16[32,128,128]{2,1,0:T(8,128)(2,1)S(1)} all-to-all(bf16[32,128,128]{2,1,0:T(8,128)(2,1)S(1)} %scatter_fusion.2), channel_id=1, replica_groups=mesh['dom'=8,'sub'=4] {'dom','sub'}, dimensions={0} | all-to-all | bytes 2097152 | tf_op jit(solution)/shard_map/all_to_all | solution.py:49
  147.2 0.7 fusion.20
  147.9 1.1 reshape.58
  149.0 6.1 %fusion.14 = bf16[2048,128]{1,0:T(8,128)(2,1)S(1)} fusion(f32[2048,128]{1,0:T(8,128)} %reshape.58, bf16[2048,2048]{1,0:T(8,128)(2,1)} %param.12, bf16[2048,128]{1,0:T(8,128)(2,1)} %copy-done.3), kind=kOutput, calls=%fused_computation.30 | convolution fusion | flops 1074528256 | bytes 10485760 | tf_op jit(solution)/shard_map/dot_general | solution.py:42
  155.2 0.8 copy-done.4
  156.0 0.7 gather_fusion.4
  156.7 0.4 select_convert_fusion
  157.1 1.3 broadcast_in_dim.51
  158.3 6.7 %scatter_fusion.3 = bf16[32,128,128]{2,1,0:T(8,128)(2,1)} fusion(bf16[32,128,128]{2,1,0:T(8,128)(2,1)} %broadcast_in_dim.51, s32[24]{0:T(128)S(1)} %get-tuple-element.15, bf16[24,128,128]{2,1,0:T(8,128)(2,1)S(1)} %select_convert_fusion), kind=kCustom, calls=%fused_computation.9 | custom fusion | flops 393216 | bytes 2359392 | tf_op jit(solution)/shard_map/scatter-add | solution.py:48
  165.0 4.5 %all-to-all-start.4 = ((bf16[32,128,128]{2,1,0:T(8,128)(2,1)}), bf16[32,128,128]{2,1,0:T(8,128)(2,1)S(1)}, u32[]{:S(2)}, u32[]{:S(2)}) async-start(bf16[32,128,128]{2,1,0:T(8,128)(2,1)} %scatter_fusion.3), calls=%async_computation.4 | async-start | bytes 2097152 | tf_op jit(solution)/shard_map/all_to_all | solution.py:49
  169.8 2.3 fusion.41
  172.1 22.3 %all-to-all-done.4 = bf16[32,128,128]{2,1,0:T(8,128)(2,1)S(1)} async-done(((bf16[32,128,128]{2,1,0:T(8,128)(2,1)}), bf16[32,128,128]{2,1,0:T(8,128)(2,1)S(1)}, u32[]{:S(2)}, u32[]{:S(2)}) %all-to-all-start.4) | async-done | bytes 1048608 | tf_op jit(solution)/shard_map/all_to_all | solution.py:49
  194.5 0.7 fusion.17
  195.2 1.2 reshape.61
  196.3 6.5 %fusion.13 = bf16[2048,128]{1,0:T(8,128)(2,1)S(1)} fusion(f32[2048,128]{1,0:T(8,128)} %reshape.61, bf16[2048,2048]{1,0:T(8,128)(2,1)} %param.12, bf16[2048,128]{1,0:T(8,128)(2,1)S(1)} %copy-done.5, bf16[2048,128]{1,0:T(8,128)(2,1)} %copy-done.3, bf16[2048,128]{1,0:T(8,128)(2,1)} %fusion.9, bf16[2048,128]{1,0:T(8,128)(2,1)} %param.8), kind=kOutput, calls=%fused_computation.29 | convolution fusion | flops 1077411840 | bytes 12058624 | tf_op jit(solution)/shard_map/dot_general | solution.py:42
  202.9 1.1 convolution_multiply_fusion.1
  204.0 0.5 fusion.8
  204.5 1.0 fusion.16
  205.5 1.1 convolution_convert_fusion
  206.6 123.9 %all-reduce.4.cloned.1.call-done = (f32[128,128]{0,1:T(8,128)}, f32[128,128]{1,0:T(8,128)}) async-done(((f32[128,128]{0,1:T(8,128)}, f32[128,128]{1,0:T(8,128)}), (f32[128,128]{0,1:T(8,128)}, f32[128,128]{1,0:T(8,128)})) %all-reduce.4.cloned.1.call-update) | async-done | bytes 131088 | tf_op jit(solution)/shard_map/psum | solution.py:72
  330.5 1.6 copy.24
  332.1 1.5 copy.55
  (26 shorter events, 1.2 us)
Async XLA Ops:
  7.2 10.9 %copy-start = (bf16[24,128,128]{2,1,0:T(8,128)(2,1)S(1)}, bf16[24,128,128]{2,1,0:T(8,128)(2,1)}, u32[]{:S(2)}) copy-start(bf16[24,128,128]{2,1,0:T(8,128)(2,1)} %param.13) | copy-start | bytes 2359300
  10.7 18.0 %all-to-all-start = ((s32[32,1,1]{2,1,0:T(1,128)}), s32[32,1,1]{2,1,0:T(1,128)S(1)}, u32[]{:S(2)}, u32[]{:S(2)}) async-start(s32[32,1,1]{2,1,0:T(1,128)} %copy.20), calls=%async_computation | async-start | bytes 32768 | tf_op jit(solution)/shard_map/all_to_all | solution.py:50
  20.9 41.6 %copy-start.2 = (bf16[2048,128]{1,0:T(8,128)(2,1)S(1)}, bf16[2048,128]{1,0:T(8,128)(2,1)}, u32[]{:S(2)}) copy-start(bf16[2048,128]{1,0:T(8,128)(2,1)} %param.8) | copy-start | bytes 1572868
  28.8 30.7 %all-to-all-start.1 = ((bf16[32,128,128]{2,1,0:T(8,128)(2,1)}), bf16[32,128,128]{2,1,0:T(8,128)(2,1)S(1)}, u32[]{:S(2)}, u32[]{:S(2)}) async-start(bf16[32,128,128]{2,1,0:T(8,128)(2,1)} %scatter_fusion), calls=%async_computation.1 | async-start | bytes 2097152 | tf_op jit(solution)/shard_map/all_to_all | solution.py:49
  112.2 0.8 copy-start.3
  149.0 20.8 %copy-start.8 = (bf16[128,128]{1,0:T(8,128)(2,1)S(1)}, bf16[128,128]{1,0:T(8,128)(2,1)}, u32[]{:S(2)}) copy-start(bf16[128,128]{1,0:T(8,128)(2,1)} %param.10) | copy-start | bytes 98308
  155.2 0.8 copy-start.4
  157.0 39.3 %copy-start.5 = (bf16[2048,128]{1,0:T(8,128)(2,1)S(1)}, bf16[2048,128]{1,0:T(8,128)(2,1)}, u32[]{:S(2)}) copy-start(bf16[2048,128]{1,0:T(8,128)(2,1)} %copy-done.4) | copy-start | bytes 1572868
  165.0 29.5 %all-to-all-start.4 = ((bf16[32,128,128]{2,1,0:T(8,128)(2,1)}), bf16[32,128,128]{2,1,0:T(8,128)(2,1)S(1)}, u32[]{:S(2)}, u32[]{:S(2)}) async-start(bf16[32,128,128]{2,1,0:T(8,128)(2,1)} %scatter_fusion.3), calls=%async_computation.4 | async-start | bytes 2097152 | tf_op jit(solution)/shard_map/all_to_all | solution.py:49
  169.6 161.0 %all-reduce.4.cloned.1.call-start = ((), (), s32[]{:S(2)}) async-start(), calls=%async_computation.5 | async-start | bytes 262144 | tf_op jit(solution)/shard_map/psum | solution.py:72
  195.2 7.7 %copy-start.6 = (f32[2048,128]{1,0:T(8,128)S(1)}, f32[2048,128]{1,0:T(8,128)}, u32[]{:S(2)}) copy-start(f32[2048,128]{1,0:T(8,128)} %fusion.41) | copy-start | bytes 3145732
  196.3 7.6 %copy-start.7 = (f32[2048,128]{1,0:T(8,128)S(1)}, f32[2048,128]{1,0:T(8,128)}, u32[]{:S(2)}) copy-start(f32[2048,128]{1,0:T(8,128)} %fusion.41) | copy-start | bytes 3145732
  196.3 7.6 %copy-start.9 = (bf16[128,128]{1,0:T(8,128)(2,1)S(1)}, bf16[128,128]{1,0:T(8,128)(2,1)}, u32[]{:S(2)}) copy-start(bf16[128,128]{1,0:T(8,128)(2,1)} %param.11) | copy-start | bytes 98308
  202.8 1.7 copy-start.1
Sparse Core Ops, SparseCore 0:
  205.7 124.8 all-reduce.3
where the time goes:
time: 342 us; the launch traced here: 340 us
  waiting for transfers between devices  171 us (50%)
  blocking collectives  58.6 us (17%)
  matrix products  36.4 us (11%)
  other arithmetic  23.4 us (7%)
  local copies, waits for them, and re-layouts  18.7 us (5%)
  starting transfers between devices  17.9 us (5%)
  between operations  14.9 us (4%)
    psum x1, waiting for transfers between devices, on_device(): totals = lax.psum((part_in, part_out), ('dom', 'sub'))  124 us
    all_to_all x2, blocking collectives, on_device(): lax.all_to_all(outbound, ('dom', 'sub'), split_axis=0, concat_axis=0, til...  58.6 us
    all_to_all x2, waiting for transfers between devices, on_device(): lax.all_to_all(outbound, ('dom', 'sub'), split_axis=0, concat_axis=0, til...  46.6 us
    dot_general x4, matrix products, on_device(): local_term = jnp.dot(inner_adj, vector, preferred_element_type=jnp.float32)  25.3 us
    scatter-add x4, other arithmetic, on_device(): outbound = empty_buffer.at[target_device].add(products)  20.5 us
    all_to_all x2, starting transfers between devices, on_device(): lax.all_to_all(outbound, ('dom', 'sub'), split_axis=0, concat_axis=0, til...  10.3 us
    all_to_all x1, starting transfers between devices, on_device(): lax.all_to_all(slot_block, ('dom', 'sub'), split_axis=0, concat_axis=0, t...  7.33 us
  transfers between devices with their start and end apart: 4, of which 3 were waited for; matrix products, arithmetic and copies ran while one was open for 4% of the time, Pallas kernels for 0%

commit v1 on v0

v1 whole, which is shorter than its diff:
```python
import functools
import math

import jax
import jax.numpy as jnp
from jax import lax
from jax.experimental import pallas as pl
from jax.experimental.pallas import tpu as pltpu
from jax.sharding import PartitionSpec as P

STEPS = 4
teleport = 0.1
MESH = pl.DeviceIdType.MESH
F32 = jnp.float32
BF16 = jnp.bfloat16


def nt_dot(a, b):
    return lax.dot_general(a, b, (((1,), (1,)), ((), ())), preferred_element_type=F32)


def tn_dot(a, b):
    return lax.dot_general(a, b, (((0,), (0,)), ((), ())), preferred_element_type=F32)


def kernel(
    n_dom, n_sub, norm_scale,
    idx_ref, up_ref, tiles_ref, ids_out, w_in_ref, w_out_ref, adj_hbm, feat_hbm,
    ig_ref, gin_ref, gout_ref,
    adj, feat, v, outb, arrived, ids_in, acc, accum, fac, act, dpre, gsend, gparts, gred, gfull,
    local_sem, send_sem, recv_sem, id_send, id_recv,
):
    n = n_dom * n_sub
    my_dom, my_sub = lax.axis_index("dom"), lax.axis_index("sub")
    me = my_dom * n_sub + my_sub
    nb, blk, width = up_ref.shape
    rows = nb * blk
    tile = min(512, rows)
    blocks = tile // blk
    far = sorted(range(n_sub), key=lambda d: -min(d, n_sub - d))

    def peer(dz, i):
        d = lax.rem(my_dom + i, n_dom)
        z = lax.rem(my_sub + dz, n_sub)
        return d, z, d * n_sub + z

    def each_peer(fn):
        for dz in far:
            def body(i, carry, dz=dz):
                fn(*peer(dz, i))
                return carry
            lax.fori_loop(1 if dz == 0 else 0, n_dom, body, 0)

    adj_copy = pltpu.make_async_copy(adj_hbm, adj, local_sem.at[0])
    feat_copy = pltpu.make_async_copy(feat_hbm, feat, local_sem.at[1])
    adj_copy.start()
    feat_copy.start()

    barrier = pltpu.get_barrier_semaphore()
    each_peer(lambda d, z, t: pl.semaphore_signal(
        barrier, inc=1, device_id=(d, z), device_id_type=MESH))
    pl.semaphore_wait(barrier, n - 1)

    def id_copy(d, z, t, slot):
        return pltpu.make_async_remote_copy(
            src_ref=ids_out.at[t], dst_ref=ids_in.at[slot], send_sem=id_send.at[t],
            recv_sem=id_recv.at[slot], device_id=(d, z), device_id_type=MESH)

    def block_copy(p, d, z, t, slot):
        return pltpu.make_async_remote_copy(
            src_ref=outb.at[p, t], dst_ref=arrived.at[p, slot], send_sem=send_sem.at[p, t],
            recv_sem=recv_sem.at[p, slot], device_id=(d, z), device_id_type=MESH)

    each_peer(lambda d, z, t: id_copy(d, z, t, me).start())
    v[...] = up_ref[...]
    accum[...] = jnp.zeros_like(accum)

    for step in range(STEPS):
        p = step % 2

        def send(d, z, t):
            if step >= 2:
                block_copy(p, d, z, t, t).wait_send()
            product = jnp.dot(tiles_ref[idx_ref[1, t]], v[idx_ref[0, t]], preferred_element_type=F32)
            outb[p, t] = product.astype(BF16)
            block_copy(p, d, z, t, me).start()

        each_peer(send)

        if step == 0:
            feat_copy.wait()

            def head(i, carry):
                at = pl.ds(pl.multiple_of(i * tile, tile), tile)
                pre = jnp.dot(feat[at, :], w_in_ref[...], preferred_element_type=F32)
                gate = jax.nn.sigmoid(pre)
                act[at, :] = (pre * gate).astype(BF16)
                fac[at, :] = gate * (1.0 + pre * (1.0 - gate))
                return carry

            lax.fori_loop(0, rows // tile, head, 0)
            adj_copy.wait()

        def local(i, carry):
            at = pl.ds(pl.multiple_of(i * tile, tile), tile)
            term = jnp.dot(adj[at, :], v[...].reshape(rows, width), preferred_element_type=F32)
            ats = pl.ds(i * blocks, blocks)
            acc[ats] = term.reshape(blocks, blk, width)
            accum[ats] += teleport * v[ats].astype(F32)
            return carry

        lax.fori_loop(0, rows // tile, local, 0)

        for dz in reversed(far):
            first = 1 if dz == 0 else 0

            def arrive(i, carry):
                d, z, s = peer(dz, i)
                if step == 0:
                    id_copy(d, z, s, s).wait_recv()
                block_copy(p, d, z, s, s).wait_recv()
                return carry

            lax.fori_loop(first, n_dom, arrive, 0)

            def gather(b, carry):
                total = acc[b]
                for i in range(first, n_dom):
                    s = peer(dz, i)[2]
                    hit = ids_in[s][0:1, :] == b
                    total += jnp.where(hit, arrived[p, s].astype(F32), 0.0)
                acc[b] = total
                return carry

            lax.fori_loop(0, nb, gather, 0)

        def update(i, carry):
            ats = pl.ds(i * blocks, blocks)
            v[ats] = ((1.0 - teleport) * acc[ats]).astype(BF16)
            return carry

        lax.fori_loop(0, rows // tile, update, 0)

    def wait_sends(d, z, t):
        id_copy(d, z, t, t).wait_send()
        block_copy(0, d, z, t, t).wait_send()
        block_copy(1, d, z, t, t).wait_send()

    hid = w_in_ref.shape[1]
    feats = w_in_ref.shape[0]

    def tail(i, carry):
        part_in, part_out = carry
        at = pl.ds(pl.multiple_of(i * tile, tile), tile)
        ats = pl.ds(i * blocks, blocks)
        grad = (accum[ats] + v[ats].astype(F32)).astype(BF16).reshape(tile, width)
        part_out += tn_dot(act[at, :], grad)
        back = nt_dot(grad, w_out_ref[...])
        inner = (back * fac[at, :]).astype(BF16)
        dpre[at, :] = inner
        part_in += tn_dot(feat[at, :], inner)
        return part_in, part_out

    part_in, part_out = lax.fori_loop(
        0, rows // tile, tail,
        (jnp.zeros((feats, hid), F32), jnp.zeros((hid, width), F32)))
    chunk = gred.shape[0]
    owners = gsend.shape[0]
    gsend[0:feats // chunk] = (part_in * norm_scale).reshape(feats // chunk, chunk, hid)
    gsend[feats // chunk:owners] = (part_out * norm_scale).reshape(hid // chunk, chunk, width)
    each_peer(wait_sends)

    def part_copy(d, z, t, slot):
        return pltpu.make_async_remote_copy(
            src_ref=gsend.at[t], dst_ref=gparts.at[slot], send_sem=send_sem.at[0, t],
            recv_sem=recv_sem.at[0, slot], device_id=(d, z), device_id_type=MESH)

    def sum_copy(d, z, t, own, slot):
        return pltpu.make_async_remote_copy(
            src_ref=gred, dst_ref=gfull.at[own], send_sem=send_sem.at[1, t],
            recv_sem=recv_sem.at[1, slot], device_id=(d, z), device_id_type=MESH)

    def when_owner(t, fn):
        if owners == n:
            fn()
        else:
            pl.when(t < owners)(fn)

    each_peer(lambda d, z, t: when_owner(t, lambda: part_copy(d, z, t, me).start()))

    def input_grad(i, carry):
        at = pl.ds(pl.multiple_of(i * tile, tile), tile)
        ig_ref[at, :] = nt_dot(dpre[at, :], w_in_ref[...]).astype(BF16)
        return carry

    lax.fori_loop(0, rows // tile, input_grad, 0)

    def reduce():
        each_peer(lambda d, z, s: pltpu.make_async_remote_copy(
            src_ref=gsend.at[0], dst_ref=gparts.at[s], send_sem=send_sem.at[0, s],
            recv_sem=recv_sem.at[0, s], device_id=(d, z), device_id_type=MESH).wait_recv())
        gparts[me] = gsend[me]

        def add(i, total):
            return total + gparts[i]

        total = lax.fori_loop(1, n, add, gparts[0])
        gred[...] = total
        gfull[me] = total
        each_peer(lambda d, z, t: sum_copy(d, z, t, me, me).start())

    when_owner(me, reduce)
    each_peer(lambda d, z, t: when_owner(t, lambda: part_copy(d, z, t, t).wait_send()))
    each_peer(lambda d, z, s: when_owner(s, lambda: sum_copy(d, z, s, s, s).wait_recv()))
    when_owner(me, lambda: each_peer(lambda d, z, t: sum_copy(d, z, t, me, me).wait_send()))
    gin_ref[...] = gfull[0:feats // chunk].reshape(feats, hid)
    gout_ref[...] = gfull[feats // chunk:owners].reshape(hid, width)


def on_device(n_dom, n_sub, upstream, features, w_in, w_out, inner_adj, cut_tiles, cut_list, cut_count):
    n = n_dom * n_sub
    rows, width = upstream.shape
    entries, blk, _ = cut_tiles.shape
    nb = rows // blk
    feats, hid = w_in.shape
    live = jnp.arange(entries, dtype=jnp.int32) < cut_count[0]
    owner = cut_list[:, 1] // nb
    picked = (owner[None, :] == jnp.arange(n, dtype=jnp.int32)[:, None]) & live[None, :]
    pick = lambda x: jnp.sum(jnp.where(picked, x[None, :], 0), axis=1)
    idx = jnp.stack([pick(cut_list[:, 0]), pick(cut_list[:, 2])])
    block_id = nb + pick(cut_list[:, 1] % nb - nb)
    ids = jnp.broadcast_to(block_id[:, None, None], (n, 8, 128))
    grad_rows = feats + hid
    chunk = max(8, grad_rows // n)
    owners = grad_rows // chunk
    vmem = pl.BlockSpec(memory_space=pltpu.VMEM)
    hbm = pl.BlockSpec(memory_space=pl.ANY)
    scratch = [
        pltpu.VMEM(inner_adj.shape, BF16),
        pltpu.VMEM(features.shape, BF16),
        pltpu.VMEM((nb, blk, width), BF16),
        pltpu.VMEM((2, n, blk, width), BF16),
        pltpu.VMEM((2, n, blk, width), BF16),
        pltpu.VMEM((n, 8, 128), jnp.int32),
        pltpu.VMEM((nb, blk, width), F32),
        pltpu.VMEM((nb, blk, width), F32),
        pltpu.VMEM((rows, hid), F32),
        pltpu.VMEM((rows, hid), BF16),
        pltpu.VMEM((rows, hid), BF16),
        pltpu.VMEM((owners, chunk, hid), F32),
        pltpu.VMEM((n, chunk, hid), F32),
        pltpu.VMEM((chunk, hid), F32),
        pltpu.VMEM((owners, chunk, hid), F32),
        pltpu.SemaphoreType.DMA((2,)),
        pltpu.SemaphoreType.DMA((2, n)),
        pltpu.SemaphoreType.DMA((2, n)),
        pltpu.SemaphoreType.DMA((n,)),
        pltpu.SemaphoreType.DMA((n,)),
    ]
    return pl.pallas_call(
        functools.partial(kernel, n_dom, n_sub, 1.0 / math.sqrt(rows * n)),
        out_shape=(
            jax.ShapeDtypeStruct((rows, feats), BF16),
            jax.ShapeDtypeStruct((feats, hid), F32),
            jax.ShapeDtypeStruct((hid, width), F32),
        ),
        in_specs=[pl.BlockSpec(memory_space=pltpu.SMEM)] + [vmem] * 5 + [hbm] * 2,
        out_specs=(vmem, vmem, vmem),
        scratch_shapes=scratch,
        compiler_params=pltpu.CompilerParams(collective_id=0, has_side_effects=True),
    )(idx, upstream.reshape(nb, blk, width), cut_tiles, ids, w_in, w_out, inner_adj, features)


def solution(mesh):
    both = ("dom", "sub")
    placed = (
        P(both, None),
        P(both, None),
        P(),
        P(),
        P(both, None),
        P(both, None, None),
        P(both, None),
        P(both),
    )
    return jax.shard_map(
        functools.partial(on_device, mesh.shape["dom"], mesh.shape["sub"]),
        mesh=mesh,
        in_specs=placed,
        out_specs=(P(both, None), P(), P()),
        check_vma=False,
    )
```

time: 342 us -> 138 us (0.40)
  waiting for transfers between devices: 171 us -> 0 us
  Pallas kernels: 0 us -> 129 us
  blocking collectives: 58.6 us -> 0 us
  matrix products: 36.4 us -> 0 us
  other arithmetic: 23.4 us -> 1.38 us
  starting transfers between devices: 17.9 us -> 0 us
  between operations: 14.9 us -> 1.31 us
  local copies, waits for them, and re-layouts: 18.7 us -> 6.33 us
    pallas_call x0 -> x1, Pallas kernels: none -> 129 us  [on_device(): pl.pallas_call(functools.partial(kernel, n_dom, n_sub, 1.0 / math.sqrt(ro...]
    psum x1 -> x0, waiting for transfers between devices: 124 us -> none  [on_device(): totals = lax.psum((part_in, part_out), ('dom', 'sub'))]
    all_to_all x2 -> x0, blocking collectives: 58.6 us -> none  [on_device(): lax.all_to_all(outbound, ('dom', 'sub'), split_axis=0, concat_axis=0, til...]
    all_to_all x3 -> x0, waiting for transfers between devices: 46.6 us -> none  [the longest x2 46.6 us: on_device(): lax.all_to_all(outbound, ('dom', 'sub'), split_axis=0, concat_axis=0, til...]
    dot_general x17 -> x0, matrix products: 36.4 us -> none  [the longest x4 25.3 us: on_device(): local_term = jnp.dot(inner_adj, vector, preferred_element_type=jnp.float32)]
    scatter-add x5 -> x0, other arithmetic: 21.2 us -> none  [the longest x4 20.5 us: on_device(): outbound = empty_buffer.at[target_device].add(products)]
    all_to_all x3 -> x0, starting transfers between devices: 17.6 us -> none  [the longest x2 10.3 us: on_device(): lax.all_to_all(outbound, ('dom', 'sub'), split_axis=0, concat_axis=0, til...]
    gather x5 -> x0, local copies, waits for them, and re-layouts: 5.57 us -> none  [the longest x4 4.87 us: on_device(): chosen = vector.reshape(block_count, block_rows, feature_width)[read_block]]
  transfers between devices with their start and end apart: 4 -> 0, of which waited for: 3 -> 0; matrix products, arithmetic and copies ran while one was open for 4% -> 0% of each run, Pallas kernels for 0% -> 0%
where the time goes in v1:
time: 138 us
  Pallas kernels  129 us (93%)
  local copies, waits for them, and re-layouts  6.33 us (5%)
    pallas_call x1, Pallas kernels, on_device(): pl.pallas_call(functools.partial(kernel, n_dom, n_sub, 1.0 / math.sqrt(ro...  129 us
    unnamed x3, local copies, waits for them, and re-layouts  4.81 us

profile of v1, /device:TPU:0, one launch (start us, length us, event | category | flops | bytes accessed | tf_op | source)
XLA Modules:
  0.0 138.0 jit_solution(11454142826084477215)
XLA Ops:
  1.3 0.7 and_select_fusion.1
  2.0 0.8 slice_bitcast_fusion.1
  2.8 0.1 select_reduce_fusion
  2.9 0.6 pad_add_fusion.idx_ref
  3.4 0.8 broadcast_in_dim.44.ids_out
  4.2 129.0 %shard_map.103 = (bf16[2048,128]{1,0:T(8,128)(2,1)}, f32[128,128]{1,0:T(8,128)}, f32[128,128]{1,0:T(8,128)}) custom-call(s32[2,32]{1,0:T(2,128)} %pad_add_fusion.idx_ref, bf16[16,128,128]{2,1,0:T(8,128)(2,1)} %bitcast.21, bf16[24,128,128]{2,1,0:T(8,128)(2,1)} %tiles_ref.1, s32[32,8,128]{2,1,0:T(8,128)} %broadcast_in_dim.44.ids_out, ...), custom_call_target="tpu_custom_call" | custom-call | tf_op jit(solution)/shard_map/pallas_call | solution.py:260
  133.2 1.9 %copy.15 = bf16[2048,128]{1,0:T(8,128)(2,1)} copy(bf16[2048,128]{1,0:T(8,128)(2,1)} %get-tuple-element.13) | data formatting | bytes 1048576
  135.0 1.5 %copy.16 = f32[128,128]{1,0:T(8,128)} copy(f32[128,128]{1,0:T(8,128)} %get-tuple-element.14) | data formatting | bytes 131072
  136.5 1.5 %copy.17 = f32[128,128]{1,0:T(8,128)} copy(f32[128,128]{1,0:T(8,128)} %get-tuple-element.15) | data formatting | bytes 131072
  (3 shorter events, 0.0 us)

commit v2 on v1

--- a/solution.py
+++ b/solution.py
@@ -26,8 +26,8 @@
 def kernel(
     n_dom, n_sub, norm_scale,
     idx_ref, up_ref, tiles_ref, ids_out, w_in_ref, w_out_ref, adj_hbm, feat_hbm,
-    ig_ref, gin_ref, gout_ref,
-    adj, feat, v, outb, arrived, ids_in, acc, accum, fac, act, dpre, gsend, gparts, gred, gfull,
+    dpre, gfull,
+    adj, feat, v, outb, arrived, ids_in, acc, accum, fac, act, gsend, gparts, gred,
     local_sem, send_sem, recv_sem, id_send, id_recv,
 ):
     n = n_dom * n_sub
@@ -37,19 +37,33 @@
     rows = nb * blk
     tile = min(512, rows)
     blocks = tile // blk
-    far = sorted(range(n_sub), key=lambda d: -min(d, n_sub - d))
-
-    def peer(dz, i):
-        d = lax.rem(my_dom + i, n_dom)
-        z = lax.rem(my_sub + dz, n_sub)
+    paired = n_sub & (n_sub - 1) == 0
+    pairings = list(reversed(range(n_sub)))
+    arrivals = [(0, 1, n_dom)]
+    for m in pairings[:-1]:
+        arrivals += [(m, 0, n_dom // 2), (m, n_dom // 2, n_dom)]
+
+    def partner(m, sign):
+        if not paired:
+            return lax.rem(my_sub + sign * m + n_sub, n_sub)
+        z, bit = my_sub, 1
+        while bit < n_sub:
+            if m & bit:
+                z = z + bit - 2 * bit * lax.rem(my_sub // bit, 2)
+            bit *= 2
+        return z
+
+    def peer(m, i, sign=1):
+        d = lax.rem(my_dom + sign * i + n_dom, n_dom)
+        z = partner(m, sign)
         return d, z, d * n_sub + z
 
     def each_peer(fn):
-        for dz in far:
-            def body(i, carry, dz=dz):
-                fn(*peer(dz, i))
+        for m in pairings:
+            def body(i, carry, m=m):
+                fn(*peer(m, i))
                 return carry
-            lax.fori_loop(1 if dz == 0 else 0, n_dom, body, 0)
+            lax.fori_loop(1 if m == 0 else 0, n_dom, body, 0)
 
     adj_copy = pltpu.make_async_copy(adj_hbm, adj, local_sem.at[0])
     feat_copy = pltpu.make_async_copy(feat_hbm, feat, local_sem.at[1])
@@ -63,7 +77,7 @@
 
     def id_copy(d, z, t, slot):
         return pltpu.make_async_remote_copy(
-            src_ref=ids_out.at[t], dst_ref=ids_in.at[slot], send_sem=id_send.at[t],
+            src_ref=ids_out.at[t, 0:1], dst_ref=ids_in.at[slot, 0:1], send_sem=id_send.at[t],
             recv_sem=id_recv.at[slot], device_id=(d, z), device_id_type=MESH)
 
     def block_copy(p, d, z, t, slot):
@@ -111,35 +125,31 @@
 
         lax.fori_loop(0, rows // tile, local, 0)
 
-        for dz in reversed(far):
-            first = 1 if dz == 0 else 0
+        for m, first, end in arrivals:
+            last = (m, first, end) == arrivals[-1]
 
             def arrive(i, carry):
-                d, z, s = peer(dz, i)
+                d, z, s = peer(m, i, -1)
                 if step == 0:
                     id_copy(d, z, s, s).wait_recv()
                 block_copy(p, d, z, s, s).wait_recv()
                 return carry
 
-            lax.fori_loop(first, n_dom, arrive, 0)
+            lax.fori_loop(first, end, arrive, 0)
 
             def gather(b, carry):
                 total = acc[b]
-                for i in range(first, n_dom):
-                    s = peer(dz, i)[2]
-                    hit = ids_in[s][0:1, :] == b
+                for i in range(first, end):
+                    s = peer(m, i, -1)[2]
+                    hit = ids_in[s, 0:1, :] == b
                     total += jnp.where(hit, arrived[p, s].astype(F32), 0.0)
-                acc[b] = total
+                if last:
+                    v[b] = ((1.0 - teleport) * total).astype(BF16)
+                else:
+                    acc[b] = total
                 return carry
 
             lax.fori_loop(0, nb, gather, 0)
-
-        def update(i, carry):
-            ats = pl.ds(i * blocks, blocks)
-            v[ats] = ((1.0 - teleport) * acc[ats]).astype(BF16)
-            return carry
-
-        lax.fori_loop(0, rows // tile, update, 0)
 
     def wait_sends(d, z, t):
         id_copy(d, z, t, t).wait_send()
@@ -166,8 +176,8 @@
         (jnp.zeros((feats, hid), F32), jnp.zeros((hid, width), F32)))
     chunk = gred.shape[0]
     owners = gsend.shape[0]
-    gsend[0:feats // chunk] = (part_in * norm_scale).reshape(feats // chunk, chunk, hid)
-    gsend[feats // chunk:owners] = (part_out * norm_scale).reshape(hid // chunk, chunk, width)
+    gsend[0:feats // chunk] = (part_in * norm_scale).reshape(feats // chunk, chunk, hid).astype(BF16)
+    gsend[feats // chunk:owners] = (part_out * norm_scale).reshape(hid // chunk, chunk, width).astype(BF16)
     each_peer(wait_sends)
 
     def part_copy(d, z, t, slot):
@@ -188,13 +198,6 @@
 
     each_peer(lambda d, z, t: when_owner(t, lambda: part_copy(d, z, t, me).start()))
 
-    def input_grad(i, carry):
-        at = pl.ds(pl.multiple_of(i * tile, tile), tile)
-        ig_ref[at, :] = nt_dot(dpre[at, :], w_in_ref[...]).astype(BF16)
-        return carry
-
-    lax.fori_loop(0, rows // tile, input_grad, 0)
-
     def reduce():
         each_peer(lambda d, z, s: pltpu.make_async_remote_copy(
             src_ref=gsend.at[0], dst_ref=gparts.at[s], send_sem=send_sem.at[0, s],
@@ -202,9 +205,9 @@
         gparts[me] = gsend[me]
 
         def add(i, total):
-            return total + gparts[i]
-
-        total = lax.fori_loop(1, n, add, gparts[0])
+            return total + gparts[i].astype(F32)
+
+        total = lax.fori_loop(1, n, add, gparts[0].astype(F32)).astype(BF16)
         gred[...] = total
         gfull[me] = total
         each_peer(lambda d, z, t: sum_copy(d, z, t, me, me).start())
@@ -213,8 +216,14 @@
     each_peer(lambda d, z, t: when_owner(t, lambda: part_copy(d, z, t, t).wait_send()))
     each_peer(lambda d, z, s: when_owner(s, lambda: sum_copy(d, z, s, s, s).wait_recv()))
     when_owner(me, lambda: each_peer(lambda d, z, t: sum_copy(d, z, t, me, me).wait_send()))
-    gin_ref[...] = gfull[0:feats // chunk].reshape(feats, hid)
-    gout_ref[...] = gfull[feats // chunk:owners].reshape(hid, width)
+
+
+def finish(dpre_ref, w_in_ref, gfull_ref, ig_ref, gin_ref, gout_ref):
+    owners, chunk, _ = gfull_ref.shape
+    split = gin_ref.shape[0] // chunk
+    ig_ref[...] = nt_dot(dpre_ref[...], w_in_ref[...]).astype(BF16)
+    gin_ref[...] = gfull_ref[0:split].astype(F32).reshape(gin_ref.shape)
+    gout_ref[...] = gfull_ref[split:owners].astype(F32).reshape(gout_ref.shape)
 
 
 def on_device(n_dom, n_sub, upstream, features, w_in, w_out, inner_adj, cut_tiles, cut_list, cut_count):
@@ -246,29 +255,36 @@
         pltpu.VMEM((nb, blk, width), F32),
         pltpu.VMEM((rows, hid), F32),
         pltpu.VMEM((rows, hid), BF16),
-        pltpu.VMEM((rows, hid), BF16),
-        pltpu.VMEM((owners, chunk, hid), F32),
-        pltpu.VMEM((n, chunk, hid), F32),
-        pltpu.VMEM((chunk, hid), F32),
-        pltpu.VMEM((owners, chunk, hid), F32),
+        pltpu.VMEM((owners, chunk, hid), BF16),
+        pltpu.VMEM((n, chunk, hid), BF16),
+        pltpu.VMEM((chunk, hid), BF16),
         pltpu.SemaphoreType.DMA((2,)),
         pltpu.SemaphoreType.DMA((2, n)),
         pltpu.SemaphoreType.DMA((2, n)),
         pltpu.SemaphoreType.DMA((n,)),
         pltpu.SemaphoreType.DMA((n,)),
     ]
+    dpre, sums = pl.pallas_call(
+        functools.partial(kernel, n_dom, n_sub, 1.0 / math.sqrt(rows * n)),
+        out_shape=(
+            jax.ShapeDtypeStruct((rows, hid), BF16),
+            jax.ShapeDtypeStruct((owners, chunk, hid), BF16),
+        ),
+        in_specs=[pl.BlockSpec(memory_space=pltpu.SMEM)] + [vmem] * 5 + [hbm] * 2,
+        out_specs=(vmem, vmem),
+        scratch_shapes=scratch,
+        compiler_params=pltpu.CompilerParams(collective_id=0, has_side_effects=True),
+    )(idx, upstream.reshape(nb, blk, width), cut_tiles, ids, w_in, w_out, inner_adj, features)
     return pl.pallas_call(
-        functools.partial(kernel, n_dom, n_sub, 1.0 / math.sqrt(rows * n)),
+        finish,
         out_shape=(
             jax.ShapeDtypeStruct((rows, feats), BF16),
             jax.ShapeDtypeStruct((feats, hid), F32),
             jax.ShapeDtypeStruct((hid, width), F32),
         ),
-        in_specs=[pl.BlockSpec(memory_space=pltpu.SMEM)] + [vmem] * 5 + [hbm] * 2,
+        in_specs=[vmem] * 3,
         out_specs=(vmem, vmem, vmem),
-        scratch_shapes=scratch,
-        compiler_params=pltpu.CompilerParams(collective_id=0, has_side_effects=True),
-    )(idx, upstream.reshape(nb, blk, width), cut_tiles, ids, w_in, w_out, inner_adj, features)
+    )(dpre, w_in, sums)
 
 
 def solution(mesh):

time: 138 us -> 127 us (0.920)
  Pallas kernels: 129 us -> 123 us
  local copies, waits for them, and re-layouts: 6.33 us -> 1.52 us
    pallas_call x1, Pallas kernels: 129 us -> 121 us  [on_device(): pl.pallas_call(functools.partial(kernel, n_dom, n_sub, 1.0 / math.sqrt(ro...]
    unnamed x3 -> x0, local copies, waits for them, and re-layouts: 4.81 us -> none
    pallas_call x0 -> x1, Pallas kernels: none -> 2.16 us  [on_device(): pl.pallas_call(finish, out_shape=(jax.ShapeDtypeStruct((rows, feats), BF1...]
where the time goes in v2:
time: 127 us
  Pallas kernels  123 us (97%)
  local copies, waits for them, and re-layouts  1.52 us (1%)
  other arithmetic  1.38 us (1%)
  between operations  1.31 us (1%)
    pallas_call x1, Pallas kernels, on_device(): pl.pallas_call(functools.partial(kernel, n_dom, n_sub, 1.0 / math.sqrt(ro...  121 us

profile of v2, /device:TPU:0, one launch (start us, length us, event | category | flops | bytes accessed | tf_op | source)
XLA Modules:
  0.0 127.2 jit_solution(2493059461999306493)
XLA Ops:
  1.3 0.7 and_select_fusion.1
  2.0 0.8 slice_bitcast_fusion.1
  2.8 0.1 select_reduce_fusion
  2.9 0.6 pad_add_fusion.idx_ref
  3.4 0.8 broadcast_in_dim.44.ids_out
  4.2 120.8 %shard_map.103 = (bf16[2048,128]{1,0:T(8,128)(2,1)}, bf16[32,8,128]{2,1,0:T(8,128)(2,1)}) custom-call(s32[2,32]{1,0:T(2,128)} %pad_add_fusion.idx_ref, bf16[16,128,128]{2,1,0:T(8,128)(2,1)} %bitcast.21, bf16[24,128,128]{2,1,0:T(8,128)(2,1)} %tiles_ref.1, s32[32,8,128]{2,1,0:T(8,128)} %broadcast_in_dim.44.ids_out, bf16[128,128]{1,0:T(8,128)(2,1)} %w_in_ref.3, ...), custom_call_target="tpu_custom_call" | custom-call | tf_op jit(solution)/shard_map/pallas_call | solution.py:267
  125.0 2.2 %shard_map.104 = (bf16[2048,128]{1,0:T(8,128)(2,1)}, f32[128,128]{1,0:T(8,128)}, f32[128,128]{1,0:T(8,128)}) custom-call(bf16[2048,128]{1,0:T(8,128)(2,1)} %get-tuple-element.5.dpre_ref, bf16[128,128]{1,0:T(8,128)(2,1)} %w_in_ref.3, bf16[32,8,128]{2,1,0:T(8,128)(2,1)} %get-tuple-element.6.gfull_ref), custom_call_target="tpu_custom_call" | custom-call | tf_op jit(solution)/shard_map/pallas_call | solution.py:278
  (3 shorter events, 0.0 us)

commit v3 on v2

--- a/solution.py
+++ b/solution.py
@@ -41,7 +41,7 @@
     pairings = list(reversed(range(n_sub)))
     arrivals = [(0, 1, n_dom)]
     for m in pairings[:-1]:
-        arrivals += [(m, 0, n_dom // 2), (m, n_dom // 2, n_dom)]
+        arrivals += [(m, i, min(i + 2, n_dom)) for i in range(0, n_dom, 2)] if m == 1 else [(m, 0, n_dom // 2), (m, n_dom // 2, n_dom)]
 
     def partner(m, sign):
         if not paired:
@@ -77,7 +77,7 @@
 
     def id_copy(d, z, t, slot):
         return pltpu.make_async_remote_copy(
-            src_ref=ids_out.at[t, 0:1], dst_ref=ids_in.at[slot, 0:1], send_sem=id_send.at[t],
+            src_ref=ids_out.at[t], dst_ref=ids_in.at[slot], send_sem=id_send.at[t],
             recv_sem=id_recv.at[slot], device_id=(d, z), device_id_type=MESH)
 
     def block_copy(p, d, z, t, slot):
@@ -95,7 +95,7 @@
         def send(d, z, t):
             if step >= 2:
                 block_copy(p, d, z, t, t).wait_send()
-            product = jnp.dot(tiles_ref[idx_ref[1, t]], v[idx_ref[0, t]], preferred_element_type=F32)
+            product = jnp.dot(tiles_ref[idx_ref[2, t]], v[idx_ref[0, t]], preferred_element_type=F32)
             outb[p, t] = product.astype(BF16)
             block_copy(p, d, z, t, me).start()
 
@@ -149,7 +149,7 @@
                     acc[b] = total
                 return carry
 
-            lax.fori_loop(0, nb, gather, 0)
+            lax.fori_loop(0, nb, gather, 0, unroll=2)
 
     def wait_sends(d, z, t):
         id_copy(d, z, t, t).wait_send()
@@ -233,12 +233,11 @@
     nb = rows // blk
     feats, hid = w_in.shape
     live = jnp.arange(entries, dtype=jnp.int32) < cut_count[0]
-    owner = cut_list[:, 1] // nb
-    picked = (owner[None, :] == jnp.arange(n, dtype=jnp.int32)[:, None]) & live[None, :]
-    pick = lambda x: jnp.sum(jnp.where(picked, x[None, :], 0), axis=1)
-    idx = jnp.stack([pick(cut_list[:, 0]), pick(cut_list[:, 2])])
-    block_id = nb + pick(cut_list[:, 1] % nb - nb)
-    ids = jnp.broadcast_to(block_id[:, None, None], (n, 8, 128))
+    owner = jnp.where(live, cut_list[:, 1] // nb, n)
+    picked = owner[None, :] == jnp.arange(n, dtype=jnp.int32)[:, None]
+    idx = jnp.sum(jnp.where(picked[None], cut_list.T[:, None, :], 0), axis=2)
+    block_id = jnp.where(jnp.any(picked, axis=1), idx[1] % nb, nb)
+    ids = jnp.broadcast_to(block_id[:, None, None], (n, 1, 128))
     grad_rows = feats + hid
     chunk = max(8, grad_rows // n)
     owners = grad_rows // chunk
@@ -250,7 +249,7 @@
         pltpu.VMEM((nb, blk, width), BF16),
         pltpu.VMEM((2, n, blk, width), BF16),
         pltpu.VMEM((2, n, blk, width), BF16),
-        pltpu.VMEM((n, 8, 128), jnp.int32),
+        pltpu.VMEM((n, 1, 128), jnp.int32),
         pltpu.VMEM((nb, blk, width), F32),
         pltpu.VMEM((nb, blk, width), F32),
         pltpu.VMEM((rows, hid), F32),

time: 127 us -> 125 us (0.984)
  Pallas kernels: 123 us -> 121 us
    pallas_call x1, Pallas kernels: 121 us -> 119 us  [on_device(): pl.pallas_call(functools.partial(kernel, n_dom, n_sub, 1.0 / math.sqrt(ro...]
where the time goes in v3:
time: 125 us
  Pallas kernels  121 us (97%)
  other arithmetic  1.57 us (1%)
  between operations  1.3 us (1%)
    pallas_call x1, Pallas kernels, on_device(): pl.pallas_call(functools.partial(kernel, n_dom, n_sub, 1.0 / math.sqrt(ro...  119 us

profile of v3, /device:TPU:0, one launch (start us, length us, event | category | flops | bytes accessed | tf_op | source)
XLA Modules:
  0.0 125.0 jit_solution(7917198566480148707)
XLA Ops:
  1.3 0.7 compare_select_fusion.2
  2.0 0.1 fusion.2
  2.1 0.8 select_reduce_fusion.idx_ref
  2.8 0.0 copy-start
  2.9 0.7 broadcast_in_dim.40.ids_out
  3.6 0.0 copy-done
  3.6 119.3 %shard_map.103 = (bf16[2048,128]{1,0:T(8,128)(2,1)}, bf16[32,8,128]{2,1,0:T(8,128)(2,1)}) custom-call(s32[3,32]{1,0:T(4,128)} %copy-done, bf16[16,128,128]{2,1,0:T(8,128)(2,1)} %bitcast.16, bf16[24,128,128]{2,1,0:T(8,128)(2,1)} %tiles_ref.1, s32[32,1,128]{2,1,0:T(1,128)} %broadcast_in_dim.40.ids_out, bf16[128,128]{1,0:T(8,128)(2,1)} %w_in_ref.3, ...), custom_call_target="tpu_custom_call" | custom-call | tf_op jit(solution)/shard_map/pallas_call | solution.py:266
  122.9 2.2 %shard_map.104 = (bf16[2048,128]{1,0:T(8,128)(2,1)}, f32[128,128]{1,0:T(8,128)}, f32[128,128]{1,0:T(8,128)}) custom-call(bf16[2048,128]{1,0:T(8,128)(2,1)} %get-tuple-element.5.dpre_ref, bf16[128,128]{1,0:T(8,128)(2,1)} %w_in_ref.3, bf16[32,8,128]{2,1,0:T(8,128)(2,1)} %get-tuple-element.6.gfull_ref), custom_call_target="tpu_custom_call" | custom-call | tf_op jit(solution)/shard_map/pallas_call | solution.py:277
  (1 shorter events, 0.0 us)
Async XLA Ops:
  2.8 0.7 copy-start
